TPU v7x, 32 devices: a whole 2x2x4 slice. The times are simulated.
32 devices in a mesh: groups: 2 (over x), ctx: 16 (over z, y, core).
Axes of the slice: x: 2, y: 2, z: 4, core: 2. Of those that a mesh axis runs over, the one named last changes fastest.
Arguments:
- queries: bfloat16 [2048, 4096], P(('groups', 'ctx')), parts along dimension 0, may hold values from -256 to 256
- text_keys: bfloat16 [2048, 512], P(('groups', 'ctx')), parts along dimension 0, may hold values from -4 to 4
- text_values: bfloat16 [2048, 512], P(('groups', 'ctx')), parts along dimension 0, may hold values from -5 to 5
- image_features: bfloat16 [16384, 256], P(('groups', 'ctx')), parts along dimension 0, may hold values from -300 to 300
- kv_weight: bfloat16 [8192, 1024], P('ctx'), may hold values from -0.0625 to 0.0625
- image_grids: int32 [32, 3], P(('groups', 'ctx')), parts along dimension 0, may hold values from 0 to 58, as said below
Outputs:
- attention: bfloat16 [2048, 4096], P(('groups', 'ctx')), parts along dimension 0
- cache_keys: bfloat16 [2048, 512], P(('groups', 'ctx')), parts along dimension 0
- cache_values: bfloat16 [2048, 512], P(('groups', 'ctx')), parts along dimension 0
There are 2 independent parts, one for each index of `groups`. A program takes and returns all parts, laid end to end along the dimension named above; an argument that names none is the same for every part. Nothing has to cross between parts.
Inputs may be any that keep to these rules, and one draw needn't show every extreme that they name: `image_grids`: row b describes the one image of context shard b: offset o, grid rows gh and grid columns gw with 2 <= gh, gw <= 4; its tokens take positions b * 64 + o to b * 64 + o + gh * gw - 1, token k at grid row k // gw and column k % gw; o + gh * gw <= 62; some shard has a 4 x 4 image.
All inputs are finite; a program needn't handle non-finite values.
Results may differ from a plain program's by a relative error of at most 0.0053.
Values may be sent and summed in bfloat16 or wider, within the bound.
No kernel may reach another device: no remote copies, remote signals or barrier semaphores. Data moves between devices by JAX's collectives and lax.ppermute only.
A program may use at most 128 MiB of HBM per device.

v0:
```python
import math
import jax
import jax.numpy as jnp
from jax import lax
from jax.sharding import PartitionSpec as P

D = 8192
HEAD_DIM = 128
GRID = 4


def rope_tables(time_ids, height_ids, width_ids):
    half_dim = HEAD_DIM // 2
    first_bound = HEAD_DIM // 8
    second_bound = first_bound + 3 * HEAD_DIM // 16
    pair_index = jnp.arange(half_dim, dtype=jnp.int32)
    inv_freq = 1000000.0 ** (-(2.0 * pair_index.astype(jnp.float32)) / HEAD_DIM)
    chosen = jnp.where(
        pair_index[None, :] < first_bound,
        time_ids[:, None],
        jnp.where(pair_index[None, :] < second_bound, height_ids[:, None], width_ids[:, None]),
    )
    angles = chosen.astype(jnp.float32) * inv_freq[None, :]
    cosine = jnp.concatenate([jnp.cos(angles), jnp.cos(angles)], axis=1)
    sine_table = jnp.concatenate([jnp.sin(angles), jnp.sin(angles)], axis=1)
    return (cosine, sine_table)


def rotate(key_heads, cosine, sine_table):
    half_dim = HEAD_DIM // 2
    turned = jnp.concatenate([-key_heads[..., half_dim:], key_heads[..., :half_dim]], axis=-1)
    return key_heads * cosine[:, None, :] + turned * sine_table[:, None, :]


def prepare(query_rows, kv_count, head_group):
    count_rows = query_rows.shape[0]
    shaped = query_rows.reshape(count_rows, kv_count, head_group, HEAD_DIM)
    return shaped.transpose(1, 2, 0, 3).reshape(kv_count, head_group * count_rows, HEAD_DIM)


def finish(summed, totals, count_rows, kv_count, head_group):
    blended = summed / totals[..., None]
    blended = blended.reshape(kv_count, head_group, count_rows, HEAD_DIM).transpose(2, 0, 1, 3)
    return blended.reshape(count_rows, kv_count * head_group * HEAD_DIM).astype(jnp.bfloat16)


def update(carry_state, query_set, positions, block_keys, block_values, key_start):
    running_max, running_sum, running_out = carry_state
    score_scale = 1.0 / math.sqrt(HEAD_DIM)
    scores = (
        jnp.einsum("grd,kgd->grk", query_set, block_keys, preferred_element_type=jnp.float32)
        * score_scale
    )
    key_pos = key_start + jnp.arange(block_keys.shape[0], dtype=jnp.int32)
    allowed = key_pos[None, None, :] <= positions[None, :, None]
    scores = jnp.where(allowed, scores, -1e30)
    new_max = jnp.maximum(running_max, jnp.max(scores, axis=-1))
    shrink = jnp.exp(running_max - new_max)
    weight = jnp.where(allowed, jnp.exp(scores - new_max[..., None]), 0.0)
    running_sum = running_sum * shrink + jnp.sum(weight, axis=-1)
    running_out = running_out * shrink[..., None] + jnp.einsum(
        "grk,kgd->grd",
        weight.astype(jnp.bfloat16),
        block_values,
        preferred_element_type=jnp.float32,
    )
    return (new_max, running_sum, running_out)


def body(queries, text_keys, text_values, image_features, kv_weight, image_grids):
    ctx_index = lax.axis_index("ctx")
    row_count = queries.shape[0]
    kv_width = text_keys.shape[1]
    kv_count = kv_width // HEAD_DIM
    head_group = queries.shape[1] // kv_width
    slot_count = GRID * GRID
    partial_kv = lax.dot_general(
        image_features, kv_weight, (((0,), (0,)), ((), ())), preferred_element_type=jnp.float32
    )
    feature_f32 = image_features.astype(jnp.float32)
    square_sums = jnp.sum(feature_f32 * feature_f32, axis=0)
    raw_kv, power_total = (
        lax.psum_scatter(partial_kv, "ctx", scatter_dimension=0, tiled=True),
        lax.psum_scatter(square_sums, "ctx", scatter_dimension=0, tiled=True),
    )
    normed = raw_kv * lax.rsqrt(power_total / D + 1e-06)[:, None]
    offset = image_grids[0, 0]
    grid_tall = image_grids[0, 1]
    grid_wide = image_grids[0, 2]
    within = jnp.arange(slot_count, dtype=jnp.int32)
    image_start = ctx_index * row_count + offset
    time_ids = jnp.broadcast_to(image_start, (slot_count,))
    height_ids = image_start + within // grid_wide
    width_ids = image_start + within % grid_wide
    cosine, sine_table = rope_tables(time_ids, height_ids, width_ids)
    key_heads = normed[:, :kv_width].reshape(slot_count, kv_count, HEAD_DIM)
    image_keys = (
        rotate(key_heads, cosine, sine_table).reshape(slot_count, kv_width).astype(jnp.bfloat16)
    )
    image_values = normed[:, kv_width:].astype(jnp.bfloat16)
    live_slot = within < grid_tall * grid_wide
    local_rows = jnp.arange(row_count, dtype=jnp.int32)
    one_hot = ((local_rows[:, None] == offset + within[None, :]) & live_slot[None, :]).astype(
        jnp.bfloat16
    )
    image_rows = (local_rows >= offset) & (local_rows < offset + grid_tall * grid_wide)
    placed = jnp.dot(
        one_hot,
        jnp.concatenate([image_keys, image_values], axis=1),
        preferred_element_type=jnp.float32,
    ).astype(jnp.bfloat16)
    cache_keys = jnp.where(image_rows[:, None], placed[:, :kv_width], text_keys)
    cache_values = jnp.where(image_rows[:, None], placed[:, kv_width:], text_values)
    half_rows = row_count // 2
    lead_queries = queries[:half_rows]
    trail_queries = queries[half_rows:]
    trail_base = ctx_index * row_count + half_rows
    lead_base = ctx_index * row_count
    query_sets = jnp.stack(
        [prepare(lead_queries, kv_count, head_group), prepare(trail_queries, kv_count, head_group)]
    )
    query_span = head_group * half_rows
    row_pos = jnp.arange(query_span, dtype=jnp.int32) % half_rows
    base_rows = jnp.stack([lead_base, trail_base])
    query_pos = base_rows[:, None] + row_pos[None, :]
    limits = base_rows + half_rows - 1
    initial = (
        jnp.full((2, kv_count, query_span), -1e30, jnp.float32),
        jnp.zeros((2, kv_count, query_span), jnp.float32),
        jnp.zeros((2, kv_count, query_span, HEAD_DIM), jnp.float32),
    )
    piece_keys = lax.all_gather(cache_keys, "ctx", axis=0, tiled=True)
    piece_values = lax.all_gather(cache_values, "ctx", axis=0, tiled=True)
    piece_size = piece_keys.shape[0]
    block_size = math.gcd(piece_size, 512)
    block_count = piece_size // block_size
    split_keys = piece_keys.reshape(block_count, block_size, kv_count, HEAD_DIM)
    split_values = piece_values.reshape(block_count, block_size, kv_count, HEAD_DIM)

    def scan_step(carried_state, scan_item):
        block_keys, block_values, number = scan_item
        key_start = number * block_size
        outcome = []
        for half_index in range(2):
            half_state = tuple((member[half_index] for member in carried_state))
            updated = lax.cond(
                key_start <= limits[half_index],
                lambda current: update(
                    current,
                    query_sets[half_index],
                    query_pos[half_index],
                    block_keys,
                    block_values,
                    key_start,
                ),
                lambda current: current,
                half_state,
            )
            outcome.append(updated)
        stacked = tuple(
            (
                jnp.stack([outcome[0][number_index], outcome[1][number_index]])
                for number_index in range(3)
            )
        )
        return (stacked, None)

    result_state, unused_out = lax.scan(
        scan_step, initial, (split_keys, split_values, jnp.arange(block_count, dtype=jnp.int32))
    )
    running_max, running_sum, running_out = result_state
    lead_out = finish(running_out[0], running_sum[0], half_rows, kv_count, head_group)
    trail_out = finish(running_out[1], running_sum[1], half_rows, kv_count, head_group)
    attention = jnp.concatenate([lead_out, trail_out], axis=0)
    return (attention, cache_keys, cache_values)


def solution(mesh):
    in_specs = (
        P(("groups", "ctx"), None),
        P(("groups", "ctx"), None),
        P(("groups", "ctx"), None),
        P(("groups", "ctx"), None),
        P("ctx", None),
        P(("groups", "ctx"), None),
    )
    out_specs = (P(("groups", "ctx"), None), P(("groups", "ctx"), None), P(("groups", "ctx"), None))
    return jax.shard_map(body, mesh=mesh, in_specs=in_specs, out_specs=out_specs, check_vma=False)
```

profile of v0, /device:TPU:25, one launch (start us, length us, event | category | flops | bytes accessed | tf_op | source)
XLA Modules:
  0.0 195.3 jit_solution(3191314341069254623)
XLA Ops:
  7.3 1.1 copy-done
  8.4 2.4 %fusion.47 = f32[256,1024]{1,0:T(8,128)} fusion(bf16[512,256]{1,0:T(8,128)(2,1)} %param.15, bf16[512,1024]{1,0:T(8,128)(2,1)S(1)} %copy-done), kind=kOutput, calls=%fused_computation.104 | convolution fusion | flops 268435456 | bytes 2359296 | tf_op jit(solution)/shard_map/dot_general | solution.py:77
  17.4 25.9 %all-reduce = f32[256]{0:T(256)S(1)} all-reduce(f32[256]{0:T(256)S(1)} %multiply_reduce_fusion), channel_id=3, replica_groups=mesh['groups'=2,'ctx'=16] {'ctx'}, use_global_device_ids=true, to_apply=%region_2.0.clone | all-reduce | flops 256 | bytes 2048
  45.8 21.6 %reduce-scatter.2.cloned.1.call-done = f32[16,1024]{1,0:T(8,128)} async-done(((f32[256,1024]{1,0:T(8,128)}), f32[16,1024]{1,0:T(8,128)}) %reduce-scatter.2.cloned.1.call-update) | async-done | bytes 65552 | tf_op jit(solution)/shard_map/reduce_scatter | solution.py:83
  67.4 0.9 broadcast_multiply_fusion
  70.5 0.8 copy.26
  71.4 37.9 %all-gather.3.cloned.1.call-done = bf16[1024,512]{1,0:T(8,128)(2,1)} async-done(((bf16[64,512]{1,0:T(8,128)(2,1)}), bf16[1024,512]{1,0:T(8,128)(2,1)}) %all-gather.3.cloned.1.call-update) | async-done | bytes 1048592 | tf_op jit(solution)/shard_map/all_gather | solution.py:132
  109.3 2.2 %reshape.193 = bf16[2,512,4,128]{3,2,1,0:T(4,128)(2,1)} reshape(bf16[1024,512]{1,0:T(8,128)(2,1)} %all-gather.3.cloned.1.call-done) | data formatting | bytes 2097152 | tf_op jit(solution)/shard_map/reshape | solution.py:137
  111.4 37.4 %all-gather.5.cloned.1.call-done = bf16[1024,512]{1,0:T(8,128)(2,1)} async-done(((bf16[64,512]{1,0:T(8,128)(2,1)}), bf16[1024,512]{1,0:T(8,128)(2,1)}) %all-gather.5.cloned.1.call-update) | async-done | bytes 1048592 | tf_op jit(solution)/shard_map/all_gather | solution.py:133
  148.9 2.1 %reshape.194 = bf16[2,512,4,128]{3,2,1,0:T(4,128)(2,1)} reshape(bf16[1024,512]{1,0:T(8,128)(2,1)} %all-gather.5.cloned.1.call-done) | data formatting | bytes 2097152 | tf_op jit(solution)/shard_map/reshape | solution.py:138
  151.1 35.4 %while.15 = (s32[]{:T(128)}, f32[2,4,256]{2,1,0:T(4,128)S(1)}, f32[2,4,256]{2,1,0:T(4,128)S(1)}, f32[2,4,256,128]{3,2,1,0:T(8,128)S(1)}, s32[2]{0:T(128)S(1)}, /...) while((s32[]{:T(128)}, f32[2,4,256]{2,1,0:T(4,128)S(1)}, ...), condition=%wide.region_12.13_spmd.clone, body=%wide.region_3.12_spmd.clone.sunk | while | flops 551560704 | bytes 36390424 | solution.py:168
  156.5 5.1 %conditional.6 = (f32[1,4,256]{2,1,0:T(4,128)}, f32[1,4,256]{2,1,0:T(4,128)S(1)}, f32[1,4,256,128]{3,2,1,0:T(8,128)S(1)}) conditional(s32[]{:T(128)} %convert_element_type.81, (f32[4,256]{1,0:T(4,128)}, f32[4,256]{1,0:T(4,128)S(1)}, f32[4,256,128]{2,1,0:T(8,128)S(1)}) %tuple.139, (s32[]{:T(128)}, s32[2,256]{1,0:T(2,128)S(1)}, ...), branch_computations={%region_8.8_spmd, %region_9.11_spmd} | conditional | flops 275646976 | bytes 9239580 | solution.py:146
  157.8 1.5 fusion.16
  160.0 1.6 fusion.17
  162.9 5.1 %conditional.7 = (f32[1,4,256]{2,1,0:T(4,128)}, f32[1,4,256]{2,1,0:T(4,128)S(1)}, f32[1,4,256,128]{3,2,1,0:T(8,128)S(1)}) conditional(s32[]{:T(128)} %convert_element_type.82, (f32[4,256]{1,0:T(4,128)}, f32[4,256]{1,0:T(4,128)S(1)}, f32[4,256,128]{2,1,0:T(8,128)S(1)}) %tuple.141, (s32[]{:T(128)}, s32[2,256]{1,0:T(2,128)S(1)}, ...), branch_computations={%region_4.4_spmd, %region_5.7_spmd} | conditional | flops 275646976 | bytes 9239580 | solution.py:146
  164.3 1.5 fusion.4
  166.4 1.6 fusion.5
  174.2 5.1 %conditional.6 = (f32[1,4,256]{2,1,0:T(4,128)}, f32[1,4,256]{2,1,0:T(4,128)S(1)}, f32[1,4,256,128]{3,2,1,0:T(8,128)S(1)}) conditional(s32[]{:T(128)} %convert_element_type.81, (f32[4,256]{1,0:T(4,128)}, f32[4,256]{1,0:T(4,128)S(1)}, f32[4,256,128]{2,1,0:T(8,128)S(1)}) %tuple.139, (s32[]{:T(128)}, s32[2,256]{1,0:T(2,128)S(1)}, ...), branch_computations={%region_8.8_spmd, %region_9.11_spmd} | conditional | flops 275646976 | bytes 9239580 | solution.py:146
  175.5 1.5 fusion.16
  177.7 1.6 fusion.17
  180.6 5.1 %conditional.7 = (f32[1,4,256]{2,1,0:T(4,128)}, f32[1,4,256]{2,1,0:T(4,128)S(1)}, f32[1,4,256,128]{3,2,1,0:T(8,128)S(1)}) conditional(s32[]{:T(128)} %convert_element_type.82, (f32[4,256]{1,0:T(4,128)}, f32[4,256]{1,0:T(4,128)S(1)}, f32[4,256,128]{2,1,0:T(8,128)S(1)}) %tuple.141, (s32[]{:T(128)}, s32[2,256]{1,0:T(2,128)S(1)}, ...), branch_computations={%region_4.4_spmd, %region_5.7_spmd} | conditional | flops 275646976 | bytes 9239580 | solution.py:146
  182.0 1.5 fusion.4
  184.1 1.6 fusion.5
  187.9 0.8 pad_maximum_fusion.3
  (123 shorter events, 26.3 us)
Async XLA Ops:
  7.2 1.2 copy-start
  7.2 8.9 %copy-start.9 = (u32[32]{0:T(128)S(1)}, u32[32]{0:T(128)}, u32[]{:S(2)}) copy-start(u32[32]{0:T(128)} %constant.92) | copy-start | bytes 388
  7.2 10.1 %copy-start.4 = (bf16[512,256]{1,0:T(8,128)(2,1)S(1)}, bf16[512,256]{1,0:T(8,128)(2,1)}, u32[]{:S(2)}) copy-start(bf16[512,256]{1,0:T(8,128)(2,1)} %param.15) | copy-start | bytes 786436
  7.2 3.7 %copy-start.8 = (s32[1,3]{1,0:T(1,128)S(1)}, s32[1,3]{1,0:T(1,128)}, u32[]{:S(2)}) copy-start(s32[1,3]{1,0:T(1,128)} %param.17) | copy-start | bytes 40
  7.2 61.5 %copy-start.6 = (bf16[64,512]{1,0:T(8,128)(2,1)S(1)}, bf16[64,512]{1,0:T(8,128)(2,1)}, u32[]{:S(2)}) copy-start(bf16[64,512]{1,0:T(8,128)(2,1)} %param.14) | copy-start | bytes 196612
  7.2 61.5 %copy-start.7 = (bf16[64,512]{1,0:T(8,128)(2,1)S(1)}, bf16[64,512]{1,0:T(8,128)(2,1)}, u32[]{:S(2)}) copy-start(bf16[64,512]{1,0:T(8,128)(2,1)} %param.13) | copy-start | bytes 196612
  7.2 63.0 %copy-start.5 = (bf16[64,4096]{1,0:T(8,128)(2,1)S(1)}, bf16[64,4096]{1,0:T(8,128)(2,1)}, u32[]{:S(2)}) copy-start(bf16[64,4096]{1,0:T(8,128)(2,1)} %param.12) | copy-start | bytes 1572868
  7.2 60.1 %reduce-scatter.2.cloned.1.call-start = ((), (), s32[]{:S(2)}) async-start(), calls=%async_computation.1 | async-start | bytes 1114112 | tf_op jit(solution)/shard_map/reduce_scatter | solution.py:83
  10.8 98.4 %all-gather.3.cloned.1.call-start = ((), (), s32[]{:S(2)}) async-start(), calls=%async_computation.2 | async-start | bytes 1114112 | tf_op jit(solution)/shard_map/all_gather | solution.py:132
  69.5 79.4 %all-gather.5.cloned.1.call-start = ((), (), s32[]{:S(2)}) async-start(), calls=%async_computation.3 | async-start | bytes 1114112 | tf_op jit(solution)/shard_map/all_gather | solution.py:133
  153.7 1.2 copy-start.1
  153.8 1.5 copy-start.2
  155.3 1.2 copy-start.3
  171.4 1.2 copy-start.1
  171.4 1.5 copy-start.2
  173.0 1.2 copy-start.3
Sparse Core Ops, SparseCore 0:
  11.7 55.6 reduce-scatter.1
  70.1 39.1 all-gather.2
  112.0 36.8 all-gather.4
where the time goes:
time: 196 us; the launch traced here: 195 us
  waiting for transfers between devices  97.6 us (50%)
  blocking collectives  25.9 us (13%)
  other arithmetic  19.3 us (10%)
  between operations  19.2 us (10%)
  local copies, waits for them, and re-layouts  17.6 us (9%)
  matrix products  11.3 us (6%)
  loops' own time  4.18 us (2%)
    all_gather x1, waiting for transfers between devices, body(): piece_keys = lax.all_gather(cache_keys, 'ctx', axis=0, tiled=True)  37.9 us
    all_gather x1, waiting for transfers between devices, body(): piece_values = lax.all_gather(cache_values, 'ctx', axis=0, tiled=True)  37.4 us
    unnamed x1, blocking collectives  25.9 us
    reduce_scatter x1, waiting for transfers between devices, body(): lax.psum_scatter(partial_kv, 'ctx', scatter_dimension=0, tiled=True)  21.6 us
    dot_general x4, matrix products, update(): jnp.einsum('grk,kgd->grd', weight.astype(jnp.bfloat16), block_values, pre...  6.43 us
    reduce_sum x4, other arithmetic, update(): running_sum = running_sum * shrink + jnp.sum(weight, axis=-1)  5.93 us
    while x16, local copies, waits for them, and re-layouts  4.29 us
    another operation x10, other arithmetic, scan_step(): jnp.stack([outcome[0][number_index], outcome[1][number_index]])  4.27 us
  transfers between devices with their start and end apart: 3, of which 3 were waited for; matrix products, arithmetic and copies ran while one was open for 4% of the time, Pallas kernels for 0%

commit v1 on v0

--- a/solution.py
+++ b/solution.py
@@ -7,6 +7,17 @@
 D = 8192
 HEAD_DIM = 128
 GRID = 4
+
+
+def turned_line(value, axis, dim):
+    size = lax.axis_size(axis)
+    right = [(i, (i + 1) % size) for i in range(size)]
+    shards = [value]
+    for far in range(1, size):
+        shards = [lax.ppermute(shards[0], axis, right), *shards]
+    whole = jnp.concatenate(shards, axis=dim)
+    turn = (lax.axis_index(axis) + 1) * shards[-1].shape[dim]
+    return jnp.roll(whole, turn, axis=dim)
 
 
 def rope_tables(time_ids, height_ids, width_ids):
@@ -129,7 +140,7 @@
         jnp.zeros((2, kv_count, query_span), jnp.float32),
         jnp.zeros((2, kv_count, query_span, HEAD_DIM), jnp.float32),
     )
-    piece_keys = lax.all_gather(cache_keys, "ctx", axis=0, tiled=True)
+    piece_keys = turned_line(cache_keys, "ctx", 0)
     piece_values = lax.all_gather(cache_values, "ctx", axis=0, tiled=True)
     piece_size = piece_keys.shape[0]
     block_size = math.gcd(piece_size, 512)

time: 196 us -> 248 us (1.27)
  starting transfers between devices: 0.12 us -> 62.3 us
  waiting for transfers between devices: 97.6 us -> 87.5 us
    ppermute x0 -> x15, starting transfers between devices: none -> 62.2 us  [turned_line(): shards = [lax.ppermute(shards[0], axis, right), *shards]]
    all_gather x1 -> x0, waiting for transfers between devices: 37.9 us -> none  [body(): piece_keys = lax.all_gather(cache_keys, 'ctx', axis=0, tiled=True)]
    ppermute x0 -> x15, waiting for transfers between devices: none -> 22.1 us  [turned_line(): shards = [lax.ppermute(shards[0], axis, right), *shards]]
    all_gather x1, waiting for transfers between devices: 37.4 us -> 43.8 us  [body(): piece_values = lax.all_gather(cache_values, 'ctx', axis=0, tiled=True)]
  transfers between devices with their start and end apart: 3 -> 17, of which waited for: 3 -> 17; matrix products, arithmetic and copies ran while one was open for 4% -> 3% of each run, Pallas kernels for 0% -> 0%
where the time goes in v1:
time: 248 us; the launch traced here: 247 us
  waiting for transfers between devices  87.5 us (35%)
  starting transfers between devices  62.3 us (25%)
  blocking collectives  25.9 us (10%)
  between operations  19.8 us (8%)
  other arithmetic  19.4 us (8%)
  local copies, waits for them, and re-layouts  16.8 us (7%)
  matrix products  11.4 us (5%)
  loops' own time  4.22 us (2%)
    ppermute x15, starting transfers between devices, turned_line(): shards = [lax.ppermute(shards[0], axis, right), *shards]  62.2 us
    all_gather x1, waiting for transfers between devices, body(): piece_values = lax.all_gather(cache_values, 'ctx', axis=0, tiled=True)  43.8 us
    unnamed x1, blocking collectives  25.9 us
    ppermute x15, waiting for transfers between devices, turned_line(): shards = [lax.ppermute(shards[0], axis, right), *shards]  22.1 us
    reduce_scatter x1, waiting for transfers between devices, body(): lax.psum_scatter(partial_kv, 'ctx', scatter_dimension=0, tiled=True)  21.6 us
    dot_general x4, matrix products, update(): jnp.einsum('grk,kgd->grd', weight.astype(jnp.bfloat16), block_values, pre...  6.58 us
    reduce_sum x4, other arithmetic, update(): running_sum = running_sum * shrink + jnp.sum(weight, axis=-1)  5.98 us
  transfers between devices with their start and end apart: 17, of which 17 were waited for; matrix products, arithmetic and copies ran while one was open for 3% of the time, Pallas kernels for 0%

profile of v1, /device:TPU:25, one launch (start us, length us, event | category | flops | bytes accessed | tf_op | source)
XLA Modules:
  0.0 247.4 jit_solution(10676101617557000118)
XLA Ops:
  8.4 2.4 fusion.47
  17.4 25.9 %all-reduce = f32[256]{0:T(256)S(1)} all-reduce(f32[256]{0:T(256)S(1)} %multiply_reduce_fusion), channel_id=3, replica_groups=mesh['groups'=2,'ctx'=16] {'ctx'}, use_global_device_ids=true, to_apply=%region_2.0.clone | all-reduce | flops 256 | bytes 2048
  45.8 21.6 %reduce-scatter.2.cloned.1.call-done = f32[16,1024]{1,0:T(8,128)} async-done(((f32[256,1024]{1,0:T(8,128)}), f32[16,1024]{1,0:T(8,128)}) %reduce-scatter.2.cloned.1.call-update) | async-done | bytes 65552 | tf_op jit(solution)/shard_map/reduce_scatter | solution.py:94
  69.4 2.7 %collective-permute-start = (bf16[64,512]{1,0:T(8,128)(2,1)S(1)}, bf16[64,512]{1,0:T(8,128)(2,1)S(1)}, u32[]{:S(2)}, u32[]{:S(2)}) collective-permute-start(bf16[64,512]{1,0:T(8,128)(2,1)S(1)} %get-tuple-element.298), channel_id=1, source_target_pairs={{0,1},{1,2},{2,3},{3,4},{4,5},{5,6},{6,7},{7,8},{8,9},{9,10},{10,1... | collective-permute-start | bytes 196616 | tf_op jit(solution)/shard_map/ppermute | solution.py:17
  73.5 2.4 collective-permute-start.1
  79.5 2.4 collective-permute-done.2
  83.3 3.2 %collective-permute-done.3 = bf16[64,512]{1,0:T(8,128)(2,1)S(1)} collective-permute-done((bf16[64,512]{1,0:T(8,128)(2,1)S(1)}, bf16[64,512]{1,0:T(8,128)(2,1)S(1)}, u32[]{:S(2)}, u32[]{:S(2)}) %collective-permute-start.3) | collective-permute-done | bytes 65568 | tf_op jit(solution)/shard_map/ppermute | solution.py:17
  86.5 3.1 %collective-permute-start.4 = (bf16[64,512]{1,0:T(8,128)(2,1)S(1)}, bf16[64,512]{1,0:T(8,128)(2,1)S(1)}, u32[]{:S(2)}, u32[]{:S(2)}) collective-permute-start(bf16[64,512]{1,0:T(8,128)(2,1)S(1)} %collective-permute-done.3), channel_id=1, source_target_pairs={{0,1},{1,2},{2,3},{3,4},{4,5},{5,6},{6,7},{7,8},{8,9},{9,10},{10,1... | collective-permute-start | bytes 196616 | tf_op jit(solution)/shard_map/ppermute | solution.py:17
  91.1 4.9 %collective-permute-start.5 = (bf16[64,512]{1,0:T(8,128)(2,1)S(1)}, bf16[64,512]{1,0:T(8,128)(2,1)S(1)}, u32[]{:S(2)}, u32[]{:S(2)}) collective-permute-start(bf16[64,512]{1,0:T(8,128)(2,1)S(1)} %collective-permute-done.4), channel_id=1, source_target_pairs={{0,1},{1,2},{2,3},{3,4},{4,5},{5,6},{6,7},{7,8},{8,9},{9,10},{10,1... | collective-permute-start | bytes 196616 | tf_op jit(solution)/shard_map/ppermute | solution.py:17
  97.4 5.1 %collective-permute-start.6 = (bf16[64,512]{1,0:T(8,128)(2,1)S(1)}, bf16[64,512]{1,0:T(8,128)(2,1)S(1)}, u32[]{:S(2)}, u32[]{:S(2)}) collective-permute-start(bf16[64,512]{1,0:T(8,128)(2,1)S(1)} %collective-permute-done.5), channel_id=1, source_target_pairs={{0,1},{1,2},{2,3},{3,4},{4,5},{5,6},{6,7},{7,8},{8,9},{9,10},{10,1... | collective-permute-start | bytes 196616 | tf_op jit(solution)/shard_map/ppermute | solution.py:17
  103.8 5.1 %collective-permute-start.7 = (bf16[64,512]{1,0:T(8,128)(2,1)S(1)}, bf16[64,512]{1,0:T(8,128)(2,1)S(1)}, u32[]{:S(2)}, u32[]{:S(2)}) collective-permute-start(bf16[64,512]{1,0:T(8,128)(2,1)S(1)} %collective-permute-done.6), channel_id=1, source_target_pairs={{0,1},{1,2},{2,3},{3,4},{4,5},{5,6},{6,7},{7,8},{8,9},{9,10},{10,1... | collective-permute-start | bytes 196616 | tf_op jit(solution)/shard_map/ppermute | solution.py:17
  110.2 5.1 %collective-permute-start.8 = (bf16[64,512]{1,0:T(8,128)(2,1)S(1)}, bf16[64,512]{1,0:T(8,128)(2,1)S(1)}, u32[]{:S(2)}, u32[]{:S(2)}) collective-permute-start(bf16[64,512]{1,0:T(8,128)(2,1)S(1)} %collective-permute-done.7), channel_id=1, source_target_pairs={{0,1},{1,2},{2,3},{3,4},{4,5},{5,6},{6,7},{7,8},{8,9},{9,10},{10,1... | collective-permute-start | bytes 196616 | tf_op jit(solution)/shard_map/ppermute | solution.py:17
  116.6 5.1 %collective-permute-start.9 = (bf16[64,512]{1,0:T(8,128)(2,1)S(1)}, bf16[64,512]{1,0:T(8,128)(2,1)S(1)}, u32[]{:S(2)}, u32[]{:S(2)}) collective-permute-start(bf16[64,512]{1,0:T(8,128)(2,1)S(1)} %collective-permute-done.8), channel_id=1, source_target_pairs={{0,1},{1,2},{2,3},{3,4},{4,5},{5,6},{6,7},{7,8},{8,9},{9,10},{10,1... | collective-permute-start | bytes 196616 | tf_op jit(solution)/shard_map/ppermute | solution.py:17
  122.9 5.1 %collective-permute-start.10 = (bf16[64,512]{1,0:T(8,128)(2,1)S(1)}, bf16[64,512]{1,0:T(8,128)(2,1)S(1)}, u32[]{:S(2)}, u32[]{:S(2)}) collective-permute-start(bf16[64,512]{1,0:T(8,128)(2,1)S(1)} %collective-permute-done.9), channel_id=1, source_target_pairs={{0,1},{1,2},{2,3},{3,4},{4,5},{5,6},{6,7},{7,8},{8,9},{9,10},{10,1... | collective-permute-start | bytes 196616 | tf_op jit(solution)/shard_map/ppermute | solution.py:17
  129.3 5.1 %collective-permute-start.11 = (bf16[64,512]{1,0:T(8,128)(2,1)S(1)}, bf16[64,512]{1,0:T(8,128)(2,1)S(1)}, u32[]{:S(2)}, u32[]{:S(2)}) collective-permute-start(bf16[64,512]{1,0:T(8,128)(2,1)S(1)} %collective-permute-done.10), channel_id=1, source_target_pairs={{0,1},{1,2},{2,3},{3,4},{4,5},{5,6},{6,7},{7,8},{8,9},{9,10},{10,1... | collective-permute-start | bytes 196616 | tf_op jit(solution)/shard_map/ppermute | solution.py:17
  135.7 5.1 %collective-permute-start.12 = (bf16[64,512]{1,0:T(8,128)(2,1)S(1)}, bf16[64,512]{1,0:T(8,128)(2,1)S(1)}, u32[]{:S(2)}, u32[]{:S(2)}) collective-permute-start(bf16[64,512]{1,0:T(8,128)(2,1)S(1)} %collective-permute-done.11), channel_id=1, source_target_pairs={{0,1},{1,2},{2,3},{3,4},{4,5},{5,6},{6,7},{7,8},{8,9},{9,10},{10,1... | collective-permute-start | bytes 196616 | tf_op jit(solution)/shard_map/ppermute | solution.py:17
  142.1 5.2 %collective-permute-start.13 = (bf16[64,512]{1,0:T(8,128)(2,1)S(1)}, bf16[64,512]{1,0:T(8,128)(2,1)S(1)}, u32[]{:S(2)}, u32[]{:S(2)}) collective-permute-start(bf16[64,512]{1,0:T(8,128)(2,1)S(1)} %collective-permute-done.12), channel_id=1, source_target_pairs={{0,1},{1,2},{2,3},{3,4},{4,5},{5,6},{6,7},{7,8},{8,9},{9,10},{10,1... | collective-permute-start | bytes 196616 | tf_op jit(solution)/shard_map/ppermute | solution.py:17
  148.7 4.9 %collective-permute-start.14 = (bf16[64,512]{1,0:T(8,128)(2,1)S(1)}, bf16[64,512]{1,0:T(8,128)(2,1)S(1)}, u32[]{:S(2)}, u32[]{:S(2)}) collective-permute-start(bf16[64,512]{1,0:T(8,128)(2,1)S(1)} %collective-permute-done.13), channel_id=1, source_target_pairs={{0,1},{1,2},{2,3},{3,4},{4,5},{5,6},{6,7},{7,8},{8,9},{9,10},{10,1... | collective-permute-start | bytes 196616 | tf_op jit(solution)/shard_map/ppermute | solution.py:17
  156.6 43.8 %all-gather.2.cloned.1.call-done = bf16[1024,512]{1,0:T(8,128)(2,1)} async-done(((bf16[64,512]{1,0:T(8,128)(2,1)}), bf16[1024,512]{1,0:T(8,128)(2,1)}) %all-gather.2.cloned.1.call-update) | async-done | bytes 1048592 | tf_op jit(solution)/shard_map/all_gather | solution.py:144
  202.6 35.8 %while.15 = (s32[]{:T(128)}, f32[2,4,256]{2,1,0:T(4,128)S(1)}, f32[2,4,256]{2,1,0:T(4,128)S(1)}, f32[2,4,256,128]{3,2,1,0:T(8,128)S(1)}, s32[2]{0:T(128)S(1)}, /...) while((s32[]{:T(128)}, f32[2,4,256]{2,1,0:T(4,128)S(1)}, ...), condition=%wide.region_12.13_spmd.clone, body=%wide.region_3.12_spmd.clone.sunk | while | flops 551560704 | bytes 36390424 | solution.py:179
  207.9 5.2 %conditional.6 = (f32[1,4,256]{2,1,0:T(4,128)}, f32[1,4,256]{2,1,0:T(4,128)S(1)}, f32[1,4,256,128]{3,2,1,0:T(8,128)S(1)}) conditional(s32[]{:T(128)} %convert_element_type.81, (f32[4,256]{1,0:T(4,128)}, f32[4,256]{1,0:T(4,128)S(1)}, f32[4,256,128]{2,1,0:T(8,128)S(1)}) %tuple.139, (s32[]{:T(128)}, s32[2,256]{1,0:T(2,128)S(1)}, ...), branch_computations={%region_8.8_spmd, %region_9.11_spmd} | conditional | flops 275646976 | bytes 9239580 | solution.py:157
  214.5 5.2 %conditional.7 = (f32[1,4,256]{2,1,0:T(4,128)}, f32[1,4,256]{2,1,0:T(4,128)S(1)}, f32[1,4,256,128]{3,2,1,0:T(8,128)S(1)}) conditional(s32[]{:T(128)} %convert_element_type.82, (f32[4,256]{1,0:T(4,128)}, f32[4,256]{1,0:T(4,128)S(1)}, f32[4,256,128]{2,1,0:T(8,128)S(1)}) %tuple.141, (s32[]{:T(128)}, s32[2,256]{1,0:T(2,128)S(1)}, ...), branch_computations={%region_4.4_spmd, %region_5.7_spmd} | conditional | flops 275646976 | bytes 9239580 | solution.py:157
  225.8 5.2 %conditional.6 = (f32[1,4,256]{2,1,0:T(4,128)}, f32[1,4,256]{2,1,0:T(4,128)S(1)}, f32[1,4,256,128]{3,2,1,0:T(8,128)S(1)}) conditional(s32[]{:T(128)} %convert_element_type.81, (f32[4,256]{1,0:T(4,128)}, f32[4,256]{1,0:T(4,128)S(1)}, f32[4,256,128]{2,1,0:T(8,128)S(1)}) %tuple.139, (s32[]{:T(128)}, s32[2,256]{1,0:T(2,128)S(1)}, ...), branch_computations={%region_8.8_spmd, %region_9.11_spmd} | conditional | flops 275646976 | bytes 9239580 | solution.py:157
  232.4 5.2 %conditional.7 = (f32[1,4,256]{2,1,0:T(4,128)}, f32[1,4,256]{2,1,0:T(4,128)S(1)}, f32[1,4,256,128]{3,2,1,0:T(8,128)S(1)}) conditional(s32[]{:T(128)} %convert_element_type.82, (f32[4,256]{1,0:T(4,128)}, f32[4,256]{1,0:T(4,128)S(1)}, f32[4,256,128]{2,1,0:T(8,128)S(1)}) %tuple.141, (s32[]{:T(128)}, s32[2,256]{1,0:T(2,128)S(1)}, ...), branch_computations={%region_4.4_spmd, %region_5.7_spmd} | conditional | flops 275646976 | bytes 9239580 | solution.py:157
  (185 shorter events, 65.4 us)
Async XLA Ops:
  7.2 8.8 %copy-start.10 = (u32[32]{0:T(128)S(1)}, u32[32]{0:T(128)}, u32[]{:S(2)}) copy-start(u32[32]{0:T(128)} %constant.114) | copy-start | bytes 388
  7.2 10.1 %copy-start.4 = (bf16[512,256]{1,0:T(8,128)(2,1)S(1)}, bf16[512,256]{1,0:T(8,128)(2,1)}, u32[]{:S(2)}) copy-start(bf16[512,256]{1,0:T(8,128)(2,1)} %param.15) | copy-start | bytes 786436
  7.2 3.7 %copy-start.9 = (s32[1,3]{1,0:T(1,128)S(1)}, s32[1,3]{1,0:T(1,128)}, u32[]{:S(2)}) copy-start(s32[1,3]{1,0:T(1,128)} %param.17) | copy-start | bytes 40
  7.2 61.5 %copy-start.7 = (bf16[64,512]{1,0:T(8,128)(2,1)S(1)}, bf16[64,512]{1,0:T(8,128)(2,1)}, u32[]{:S(2)}) copy-start(bf16[64,512]{1,0:T(8,128)(2,1)} %param.14) | copy-start | bytes 196612
  7.2 61.5 %copy-start.8 = (bf16[64,512]{1,0:T(8,128)(2,1)S(1)}, bf16[64,512]{1,0:T(8,128)(2,1)}, u32[]{:S(2)}) copy-start(bf16[64,512]{1,0:T(8,128)(2,1)} %param.13) | copy-start | bytes 196612
  7.2 133.5 %copy-start.6 = (bf16[64,4096]{1,0:T(8,128)(2,1)S(1)}, bf16[64,4096]{1,0:T(8,128)(2,1)}, u32[]{:S(2)}) copy-start(bf16[64,4096]{1,0:T(8,128)(2,1)} %param.12) | copy-start | bytes 1572868
  7.2 60.1 %reduce-scatter.2.cloned.1.call-start = ((), (), s32[]{:S(2)}) async-start(), calls=%async_computation.1 | async-start | bytes 1114112 | tf_op jit(solution)/shard_map/reduce_scatter | solution.py:94
  10.8 189.6 %all-gather.2.cloned.1.call-start = ((), (), s32[]{:S(2)}) async-start(), calls=%async_computation.2 | async-start | bytes 1114112 | tf_op jit(solution)/shard_map/all_gather | solution.py:144
  69.4 85.9 %copy-start.5 = (bf16[64,512]{1,0:T(8,128)(2,1)}, bf16[64,512]{1,0:T(8,128)(2,1)S(1)}, u32[]{:S(2)}) copy-start(bf16[64,512]{1,0:T(8,128)(2,1)S(1)} %get-tuple-element.298) | copy-start | bytes 196612
  69.4 4.1 %collective-permute-start = (bf16[64,512]{1,0:T(8,128)(2,1)S(1)}, bf16[64,512]{1,0:T(8,128)(2,1)S(1)}, u32[]{:S(2)}, u32[]{:S(2)}) collective-permute-start(bf16[64,512]{1,0:T(8,128)(2,1)S(1)} %get-tuple-element.298), channel_id=1, source_target_pairs={{0,1},{1,2},{2,3},{3,4},{4,5},{5,6},{6,7},{7,8},{8,9},{9,10},{10,1... | collective-permute-start | bytes 196616 | tf_op jit(solution)/shard_map/ppermute | solution.py:17
  73.5 3.9 %collective-permute-start.1 = (bf16[64,512]{1,0:T(8,128)(2,1)S(1)}, bf16[64,512]{1,0:T(8,128)(2,1)S(1)}, u32[]{:S(2)}, u32[]{:S(2)}) collective-permute-start(bf16[64,512]{1,0:T(8,128)(2,1)S(1)} %collective-permute-done), channel_id=1, source_target_pairs={{0,1},{1,2},{2,3},{3,4},{4,5},{5,6},{6,7},{7,8},{8,9},{9,10},{10,1... | collective-permute-start | bytes 196616 | tf_op jit(solution)/shard_map/ppermute | solution.py:17
  77.3 4.6 %collective-permute-start.2 = (bf16[64,512]{1,0:T(8,128)(2,1)S(1)}, bf16[64,512]{1,0:T(8,128)(2,1)S(1)}, u32[]{:S(2)}, u32[]{:S(2)}) collective-permute-start(bf16[64,512]{1,0:T(8,128)(2,1)S(1)} %collective-permute-done.1), channel_id=1, source_target_pairs={{0,1},{1,2},{2,3},{3,4},{4,5},{5,6},{6,7},{7,8},{8,9},{9,10},{10,1... | collective-permute-start | bytes 196616 | tf_op jit(solution)/shard_map/ppermute | solution.py:17
  81.9 4.6 %collective-permute-start.3 = (bf16[64,512]{1,0:T(8,128)(2,1)S(1)}, bf16[64,512]{1,0:T(8,128)(2,1)S(1)}, u32[]{:S(2)}, u32[]{:S(2)}) collective-permute-start(bf16[64,512]{1,0:T(8,128)(2,1)S(1)} %collective-permute-done.2), channel_id=1, source_target_pairs={{0,1},{1,2},{2,3},{3,4},{4,5},{5,6},{6,7},{7,8},{8,9},{9,10},{10,1... | collective-permute-start | bytes 196616 | tf_op jit(solution)/shard_map/ppermute | solution.py:17
  86.5 4.6 %collective-permute-start.4 = (bf16[64,512]{1,0:T(8,128)(2,1)S(1)}, bf16[64,512]{1,0:T(8,128)(2,1)S(1)}, u32[]{:S(2)}, u32[]{:S(2)}) collective-permute-start(bf16[64,512]{1,0:T(8,128)(2,1)S(1)} %collective-permute-done.3), channel_id=1, source_target_pairs={{0,1},{1,2},{2,3},{3,4},{4,5},{5,6},{6,7},{7,8},{8,9},{9,10},{10,1... | collective-permute-start | bytes 196616 | tf_op jit(solution)/shard_map/ppermute | solution.py:17
  91.1 6.3 %collective-permute-start.5 = (bf16[64,512]{1,0:T(8,128)(2,1)S(1)}, bf16[64,512]{1,0:T(8,128)(2,1)S(1)}, u32[]{:S(2)}, u32[]{:S(2)}) collective-permute-start(bf16[64,512]{1,0:T(8,128)(2,1)S(1)} %collective-permute-done.4), channel_id=1, source_target_pairs={{0,1},{1,2},{2,3},{3,4},{4,5},{5,6},{6,7},{7,8},{8,9},{9,10},{10,1... | collective-permute-start | bytes 196616 | tf_op jit(solution)/shard_map/ppermute | solution.py:17
  97.4 6.4 %collective-permute-start.6 = (bf16[64,512]{1,0:T(8,128)(2,1)S(1)}, bf16[64,512]{1,0:T(8,128)(2,1)S(1)}, u32[]{:S(2)}, u32[]{:S(2)}) collective-permute-start(bf16[64,512]{1,0:T(8,128)(2,1)S(1)} %collective-permute-done.5), channel_id=1, source_target_pairs={{0,1},{1,2},{2,3},{3,4},{4,5},{5,6},{6,7},{7,8},{8,9},{9,10},{10,1... | collective-permute-start | bytes 196616 | tf_op jit(solution)/shard_map/ppermute | solution.py:17
  103.8 6.4 %collective-permute-start.7 = (bf16[64,512]{1,0:T(8,128)(2,1)S(1)}, bf16[64,512]{1,0:T(8,128)(2,1)S(1)}, u32[]{:S(2)}, u32[]{:S(2)}) collective-permute-start(bf16[64,512]{1,0:T(8,128)(2,1)S(1)} %collective-permute-done.6), channel_id=1, source_target_pairs={{0,1},{1,2},{2,3},{3,4},{4,5},{5,6},{6,7},{7,8},{8,9},{9,10},{10,1... | collective-permute-start | bytes 196616 | tf_op jit(solution)/shard_map/ppermute | solution.py:17
  110.2 6.4 %collective-permute-start.8 = (bf16[64,512]{1,0:T(8,128)(2,1)S(1)}, bf16[64,512]{1,0:T(8,128)(2,1)S(1)}, u32[]{:S(2)}, u32[]{:S(2)}) collective-permute-start(bf16[64,512]{1,0:T(8,128)(2,1)S(1)} %collective-permute-done.7), channel_id=1, source_target_pairs={{0,1},{1,2},{2,3},{3,4},{4,5},{5,6},{6,7},{7,8},{8,9},{9,10},{10,1... | collective-permute-start | bytes 196616 | tf_op jit(solution)/shard_map/ppermute | solution.py:17
  116.6 6.4 %collective-permute-start.9 = (bf16[64,512]{1,0:T(8,128)(2,1)S(1)}, bf16[64,512]{1,0:T(8,128)(2,1)S(1)}, u32[]{:S(2)}, u32[]{:S(2)}) collective-permute-start(bf16[64,512]{1,0:T(8,128)(2,1)S(1)} %collective-permute-done.8), channel_id=1, source_target_pairs={{0,1},{1,2},{2,3},{3,4},{4,5},{5,6},{6,7},{7,8},{8,9},{9,10},{10,1... | collective-permute-start | bytes 196616 | tf_op jit(solution)/shard_map/ppermute | solution.py:17
  122.9 6.4 %collective-permute-start.10 = (bf16[64,512]{1,0:T(8,128)(2,1)S(1)}, bf16[64,512]{1,0:T(8,128)(2,1)S(1)}, u32[]{:S(2)}, u32[]{:S(2)}) collective-permute-start(bf16[64,512]{1,0:T(8,128)(2,1)S(1)} %collective-permute-done.9), channel_id=1, source_target_pairs={{0,1},{1,2},{2,3},{3,4},{4,5},{5,6},{6,7},{7,8},{8,9},{9,10},{10,1... | collective-permute-start | bytes 196616 | tf_op jit(solution)/shard_map/ppermute | solution.py:17
  129.3 6.4 %collective-permute-start.11 = (bf16[64,512]{1,0:T(8,128)(2,1)S(1)}, bf16[64,512]{1,0:T(8,128)(2,1)S(1)}, u32[]{:S(2)}, u32[]{:S(2)}) collective-permute-start(bf16[64,512]{1,0:T(8,128)(2,1)S(1)} %collective-permute-done.10), channel_id=1, source_target_pairs={{0,1},{1,2},{2,3},{3,4},{4,5},{5,6},{6,7},{7,8},{8,9},{9,10},{10,1... | collective-permute-start | bytes 196616 | tf_op jit(solution)/shard_map/ppermute | solution.py:17
  135.7 6.4 %collective-permute-start.12 = (bf16[64,512]{1,0:T(8,128)(2,1)S(1)}, bf16[64,512]{1,0:T(8,128)(2,1)S(1)}, u32[]{:S(2)}, u32[]{:S(2)}) collective-permute-start(bf16[64,512]{1,0:T(8,128)(2,1)S(1)} %collective-permute-done.11), channel_id=1, source_target_pairs={{0,1},{1,2},{2,3},{3,4},{4,5},{5,6},{6,7},{7,8},{8,9},{9,10},{10,1... | collective-permute-start | bytes 196616 | tf_op jit(solution)/shard_map/ppermute | solution.py:17
  142.1 6.6 %collective-permute-start.13 = (bf16[64,512]{1,0:T(8,128)(2,1)S(1)}, bf16[64,512]{1,0:T(8,128)(2,1)S(1)}, u32[]{:S(2)}, u32[]{:S(2)}) collective-permute-start(bf16[64,512]{1,0:T(8,128)(2,1)S(1)} %collective-permute-done.12), channel_id=1, source_target_pairs={{0,1},{1,2},{2,3},{3,4},{4,5},{5,6},{6,7},{7,8},{8,9},{9,10},{10,1... | collective-permute-start | bytes 196616 | tf_op jit(solution)/shard_map/ppermute | solution.py:17
  148.7 6.2 %collective-permute-start.14 = (bf16[64,512]{1,0:T(8,128)(2,1)S(1)}, bf16[64,512]{1,0:T(8,128)(2,1)S(1)}, u32[]{:S(2)}, u32[]{:S(2)}) collective-permute-start(bf16[64,512]{1,0:T(8,128)(2,1)S(1)} %collective-permute-done.13), channel_id=1, source_target_pairs={{0,1},{1,2},{2,3},{3,4},{4,5},{5,6},{6,7},{7,8},{8,9},{9,10},{10,1... | collective-permute-start | bytes 196616 | tf_op jit(solution)/shard_map/ppermute | solution.py:17
  (7 other events, 9.2 us)
Sparse Core Ops, SparseCore 0:
  11.7 55.6 reduce-scatter.1
  153.8 46.5 all-gather.1
